TPU v7x, 32 devices: a whole 2x2x4 slice. The times are simulated.
32 devices in a mesh: groups: 2 (over x), modes: 16 (over z, y, core).
Axes of the slice: x: 2, y: 2, z: 4, core: 2. Of those that a mesh axis runs over, the one named last changes fastest.
Arguments:
- mode_fields: bfloat16 [256, 256, 2048], P(('groups', 'modes')), parts along dimension 0, may hold values from -0.59765625 to 0.59765625
- coeff: float32 [256], P('groups'), parts along dimension 0, may hold values from -6 to 6
- eigen: float32 [256], P('groups'), parts along dimension 0, may hold values from 0.1 to 100
- map_friction: float32 [512, 2048], P(('groups', 'modes')), parts along dimension 0, may hold values from 1 to 2.5
- bed: float32 [512, 2048], P(('groups', 'modes')), parts along dimension 0, may hold values from -5 to 5
- smb: float32 [512, 2048], P(('groups', 'modes')), parts along dimension 0, may hold values from -0.6 to 0.4
- thickness: float32 [512, 2048], P(('groups', 'modes')), parts along dimension 0, may hold values from 1.9 to 2.6
Outputs:
- log_friction: float32 [512, 2048], P(('groups', 'modes')), parts along dimension 0
- final_thickness: float32 [512, 2048], P(('groups', 'modes')), parts along dimension 0
There are 2 independent parts, one for each index of `groups`. A program takes and returns all parts, laid end to end along the dimension named above; each array names one. Nothing has to cross between parts.
All inputs are finite; a program needn't handle non-finite values.
Results may differ from a plain program's by a relative error of at most 0.0014.
Values may be sent and summed in bfloat16 or wider, within the bound.
A program may use at most 64 MiB of HBM per device.

v0:
```python
import functools

import jax
import jax.numpy as jnp
from jax import lax
from jax.experimental import pallas as pl
from jax.experimental.pallas import tpu as pltpu
from jax.sharding import PartitionSpec as P

STEPS = 8

flow_rate = 0.02
slide_rate = 0.1
diff_cap = 0.5
time_step = 0.4

WIRE = jnp.bfloat16
PAD = 8
LANES = 128
GROUP = 4
F32 = jnp.float32


def kernel(
    n,
    coeff_hbm, eigen_hbm, map_hbm, bed_hbm, smb_hbm, h0_hbm, fields_ref,
    logf_hbm, final_hbm,
    coeff_ref, eigen_ref, map_ref, bed_ref, smb_ref, h0_ref, logf_ref, final_ref, in_sem, out_sem,
    mf, p1out, p1own, p1in, s2out, s2in, s3out, s3in, acc,
    st_out, st_in, f_out, f_in,
    ext_b, ext_e, ext_m, ext_h, ext_d, ext_g, ext_s0, ext_s1,
    mf_sem, p1s, p1r, s2s, s2r, s3s, s3r, hs, hr,
):
    me = lax.axis_index("modes")
    c = me % 2
    a = (me // 2) % 2
    b = me // 4
    B = n // 4
    mode_dev = fields_ref.shape[0]
    rows, cols = map_ref.shape
    ks = list(range(1, B)) + [0]

    def bk(k):
        return lax.rem(b + k, B)

    def dest(k, aa, cc):
        return (bk(k) * 2 + aa) * 2 + cc

    order = [(k, aa, cc) for aa in (1, 0) for k in ks for cc in (1, 0)]

    def dest_of(k, aa, cc):
        return dest(k, a + aa - 2 * a * aa, c + cc - 2 * c * cc)

    def load(i):
        k, aa, cc = order[i]
        rr = pl.ds(pl.multiple_of(dest_of(k, aa, cc) * rows, rows), rows)
        return pltpu.make_async_copy(fields_ref.at[:, rr, :], mf.at[:, pl.ds(i * rows, rows), :], mf_sem.at[i])

    hbm = (bed_hbm, smb_hbm, h0_hbm, coeff_hbm, eigen_hbm, map_hbm)
    own = (bed_ref, smb_ref, h0_ref, coeff_ref, eigen_ref, map_ref)
    takes = [pltpu.make_async_copy(x, y, in_sem.at[i]) for i, (x, y) in enumerate(zip(hbm, own))]
    gives = [pltpu.make_async_copy(x, y, out_sem.at[i]) for i, (x, y) in enumerate(((logf_ref, logf_hbm), (final_ref, final_hbm)))]
    for take in takes:
        take.start()
    for i in range(n):
        load(i).start()

    left, right = lax.rem(me + n - 1, n), lax.rem(me + 1, n)
    core_peer = me + 1 - 2 * c
    y_peer = me + 2 - 4 * a
    barrier = pltpu.get_barrier_semaphore()

    def z_peer(k):
        return dest(k, a, c)

    for peer in [left, right, core_peer, y_peer] + [z_peer(k) for k in range(1, B)]:
        pl.semaphore_signal(barrier, inc=1, device_id={"modes": peer}, device_id_type=pl.DeviceIdType.MESH)

    for take in takes:
        take.wait()
    w = coeff_ref[...] / jnp.sqrt(1.0 + eigen_ref[...])
    w = w.astype(jnp.bfloat16).astype(F32)
    lane = lax.broadcasted_iota(jnp.int32, w.shape, 1)
    ws = []
    for j in range(mode_dev):
        picked = jnp.where(lane == me * mode_dev + j, w, 0.0)
        ws.append(jnp.sum(picked, axis=1, keepdims=True))
    st_out[0] = bed_ref[...].astype(jnp.bfloat16)
    st_out[1] = smb_ref[...].astype(jnp.bfloat16)
    st_out[2] = h0_ref[...].astype(jnp.bfloat16)

    pl.semaphore_wait(barrier, 4 + B - 1)

    def remote(src, dst, ssem, rsem, peer):
        return pltpu.make_async_remote_copy(
            src_ref=src, dst_ref=dst, send_sem=ssem, recv_sem=rsem,
            device_id={"modes": peer}, device_id_type=pl.DeviceIdType.MESH)

    def halo(kind, side):
        src = (st_out, f_out)[kind]
        dst = (st_in, f_in)[kind]
        peer = right if side == 0 else left
        at = kind * 2 + side
        return remote(src, dst.at[side], hs.at[at], hr.at[at], peer)

    has_up, has_down = me > 0, me < n - 1

    def start_halo(kind):
        @pl.when(has_down)
        def _():
            halo(kind, 0).start()

        @pl.when(has_up)
        def _():
            halo(kind, 1).start()

    def wait_halo(kind):
        @pl.when(has_down)
        def _():
            halo(kind, 0).wait_send()
            halo(kind, 1).wait_recv()

        @pl.when(has_up)
        def _():
            halo(kind, 1).wait_send()
            halo(kind, 0).wait_recv()


    CT = min(512, cols)

    def col_loop(body):
        def step(j, carry):
            body(pl.ds(pl.multiple_of(j * CT, CT), CT))
            return carry
        lax.fori_loop(0, cols // CT, step, 0)

    def partial(i, out):
        load(i).wait()

        def body(cs):
            tot = None
            for j in range(mode_dev):
                term = mf[j, pl.ds(i * rows, rows), cs].astype(F32) * ws[j]
                tot = term if tot is None else tot + term
            out[:, cs] = tot
        col_loop(body)

    def s1copy(m):
        return remote(p1out.at[m], p1in.at[m], p1s.at[m], p1r.at[m], core_peer)

    def stage1(m):
        partial(2 * m, p1out.at[m])
        s1copy(m).start()
        partial(2 * m + 1, p1own.at[m])

    def s2copy(q):
        return remote(s2out.at[q], s2in.at[q], s2s.at[q], s2r.at[q], y_peer)

    def stage2(q):
        s1copy(q).wait_recv()

        def body(cs):
            s2out[q, :, cs] = (p1own[q, :, cs] + p1in[q, :, cs]).astype(WIRE)
        col_loop(body)
        s2copy(q).start()

    def s3copy(q):
        return remote(s3out.at[q], s3in.at[q], s3s.at[q], s3r.at[q], z_peer(ks[q]))

    def stage3(q):
        m = B + q
        s1copy(m).wait_recv()
        s2copy(q).wait_recv()

        def body(cs):
            tot = p1own[m, :, cs] + p1in[m, :, cs] + s2in[q, :, cs].astype(F32)
            if ks[q]:
                s3out[q, :, cs] = tot.astype(WIRE)
            else:
                acc[:, cs] = tot + map_ref[:, cs]
        col_loop(body)
        if ks[q]:
            s3copy(q).start()

    for q in range(B):
        stage1(q)
        if q:
            stage2(q - 1)
    stage1(B)
    stage2(B - 1)
    for q in range(1, B):
        stage1(B + q)
    for q in range(B):
        stage3(q)
    start_halo(0)
    for q in range(B - 1):
        s3copy(q).wait_recv()

    def finish(cs):
        tot = acc[:, cs]
        for q in range(B - 1):
            tot = tot + s3in[q, :, cs].astype(F32)
        logf_ref[:, cs] = tot
        f_out[:, cs] = tot.astype(jnp.bfloat16)
    col_loop(finish)
    start_halo(1)
    gives[0].start()

    tiles = cols // LANES
    top, mid, low = pl.ds(PAD, rows), pl.ds(PAD + rows, rows), pl.ds(PAD + 2 * rows, rows)
    whole = 3 * rows + 2 * PAD

    def clear(ref, where, size):
        for j in range(tiles):
            ref[j + 1, where, :] = jnp.zeros((size, LANES), F32)

    for ref in (ext_s0, ext_s1, ext_d):
        clear(ref, pl.ds(0, PAD), PAD)
        clear(ref, pl.ds(PAD + 3 * rows, PAD), PAD)
        for j in (0, tiles + 1):
            ref[j] = jnp.zeros((whole, LANES), F32)
    ext_g[0] = jnp.zeros((whole, LANES), F32)

    def lanes(j):
        return slice(j * LANES, (j + 1) * LANES)

    for j in range(tiles):
        bb, hh = bed_ref[:, lanes(j)], h0_ref[:, lanes(j)]
        ext_b[j + 1, mid, :] = bb
        ext_m[j + 1, mid, :] = time_step * smb_ref[:, lanes(j)]
        ext_h[j + 1, mid, :] = hh
        ext_s0[j + 1, mid, :] = bb + hh
        ext_e[j + 1, mid, :] = slide_rate * jnp.exp(-logf_ref[:, lanes(j)])
    wait_halo(0)

    def fill(side, where, present):
        @pl.when(present)
        def _():
            for j in range(tiles):
                bb = st_in[side, 0, :, lanes(j)].astype(F32)
                hh = st_in[side, 2, :, lanes(j)].astype(F32)
                ext_b[j + 1, where, :] = bb
                ext_m[j + 1, where, :] = time_step * st_in[side, 1, :, lanes(j)].astype(F32)
                ext_h[j + 1, where, :] = hh
                ext_s0[j + 1, where, :] = bb + hh

        @pl.when(jnp.logical_not(present))
        def _():
            for ref in (ext_s0, ext_s1, ext_d):
                clear(ref, where, rows)
    fill(0, top, has_up)
    fill(1, low, has_down)
    wait_halo(1)

    def fill_e(side, where, present):
        @pl.when(present)
        def _():
            for j in range(tiles):
                ext_e[j + 1, where, :] = slide_rate * jnp.exp(-f_in[side, :, lanes(j)].astype(F32))
    fill_e(0, top, has_up)
    fill_e(1, low, has_down)

    for m in range(2 * B):
        s1copy(m).wait_send()
    for q in range(B):
        s2copy(q).wait_send()
        if ks[q]:
            s3copy(q).wait_send()

    margin = rows - 2 * STEPS

    def sweep(first, last, body):
        for lo, hi, present in ((0, rows, has_up), (rows, 2 * rows, None), (2 * rows, 3 * rows, has_down)):
            lo, hi = max(lo, first // 8 * 8), min(hi, -(-last // 8) * 8)
            if lo >= hi:
                continue
            if present is None:
                body(PAD + lo, hi - lo)
            else:
                pl.when(present)(functools.partial(body, PAD + lo, hi - lo))

    for t in range(1, STEPS + 1):
        s_ref, s_new = (ext_s0, ext_s1) if t % 2 else (ext_s1, ext_s0)
        lo_h = margin + 2 * t

        lane = lax.broadcasted_iota(jnp.int32, (1, 8, LANES), 2)
        first_lane, last_lane = lane == 0, lane == LANES - 1

        def d_rows(r, size):
            for at in range(r, r + size, 8):
                here, up, down = (slice(at + o, at + o + 8) for o in (0, -1, 1))
                for j in range(1, tiles + 1, GROUP):
                    now, later, sooner = (slice(j + o, j + o + GROUP) for o in (0, 1, -1))
                    s = s_ref[now, here, :]
                    right = pltpu.roll(jnp.where(first_lane, s_ref[later, here, :], s), LANES - 1, 2)
                    left_ = pltpu.roll(jnp.where(last_lane, s_ref[sooner, here, :], s), 1, 2)
                    gx = s_ref[now, down, :] - s_ref[now, up, :]
                    gy = right - left_
                    h = ext_h[now, here, :]
                    sq = h * h
                    d = sq * ((0.25 * flow_rate) * (sq * h) * (gx * gx + gy * gy) + ext_e[now, here, :])
                    ext_d[now, here, :] = jnp.minimum(d, diff_cap)
                    ext_g[now, here, :] = right - s

        def h_rows(r, size):
            for at in range(r, r + size, 8):
                here, up, down = (slice(at + o, at + o + 8) for o in (0, -1, 1))
                edge = pltpu.roll(ext_d[1:2, here, :] * s_ref[1:2, here, :], LANES - 1, 2)
                for j in range(1, tiles + 1, GROUP):
                    now, later = (slice(j + o, j + o + GROUP) for o in (0, 1))
                    s, d = s_ref[now, here, :], ext_d[now, here, :]
                    right = pltpu.roll(jnp.where(first_lane, ext_d[later, here, :], d), LANES - 1, 2)
                    flux = (right + d) * ext_g[now, here, :]
                    sooner = jnp.concatenate([edge, flux[:-1]], axis=0)
                    edge = flux[-1:]
                    div = (ext_d[now, down, :] + d) * (s_ref[now, down, :] - s)
                    div += (ext_d[now, up, :] + d) * (s_ref[now, up, :] - s)
                    div += flux - pltpu.roll(jnp.where(last_lane, sooner, flux), 1, 2)
                    h = jnp.maximum(ext_h[now, here, :] + ((0.5 * time_step) * div + ext_m[now, here, :]), 0.0)
                    ext_h[now, here, :] = h
                    if t < STEPS:
                        s_new[now, here, :] = ext_b[now, here, :] + h

        sweep(lo_h - 1, 3 * rows - lo_h + 1, d_rows)
        sweep(lo_h, 3 * rows - lo_h, h_rows)

    for j in range(tiles):
        final_ref[:, lanes(j)] = ext_h[j + 1, mid, :]
    gives[1].start()
    gives[0].wait()
    gives[1].wait()


def per_device(n, mode_fields, coeff, eigen, map_friction, bed, smb, thickness):
    rows, cols = map_friction.shape
    mode_dev = mode_fields.shape[0]
    B = n // 4
    modes = coeff.shape[0]
    anywhere = pl.BlockSpec(memory_space=pl.ANY)
    strip = (rows, cols)
    ext = (cols // LANES + 2, 3 * rows + 2 * PAD, LANES)
    bf = jnp.bfloat16
    dma = pltpu.SemaphoreType.DMA
    return pl.pallas_call(
        functools.partial(kernel, n),
        out_shape=(jax.ShapeDtypeStruct(strip, F32),) * 2,
        in_specs=[anywhere] * 7,
        out_specs=(anywhere, anywhere),
        scratch_shapes=[
            pltpu.VMEM((1, modes), F32),
            pltpu.VMEM((1, modes), F32),
        ] + [pltpu.VMEM(strip, F32)] * 6 + [
            dma((6,)),
            dma((2,)),
            pltpu.VMEM((mode_dev, n * rows, cols), bf),
            pltpu.VMEM((2 * B,) + strip, F32),
            pltpu.VMEM((2 * B,) + strip, F32),
            pltpu.VMEM((2 * B,) + strip, F32),
            pltpu.VMEM((B,) + strip, WIRE),
            pltpu.VMEM((B,) + strip, WIRE),
            pltpu.VMEM((B,) + strip, WIRE),
            pltpu.VMEM((B,) + strip, WIRE),
            pltpu.VMEM(strip, F32),
            pltpu.VMEM((3,) + strip, bf),
            pltpu.VMEM((2, 3) + strip, bf),
            pltpu.VMEM(strip, bf),
            pltpu.VMEM((2,) + strip, bf),
        ] + [pltpu.VMEM(ext, F32)] * 8 + [
            dma((n,)), dma((2 * B,)), dma((2 * B,)), dma((B,)), dma((B,)), dma((B,)), dma((B,)), dma((4,)), dma((4,)),
        ],
        compiler_params=pltpu.CompilerParams(collective_id=0, has_side_effects=True, vmem_limit_bytes=60 * 2**20),
        name="posterior_ice",
    )(coeff.reshape(1, modes), eigen.reshape(1, modes), map_friction, bed, smb, thickness, mode_fields)


def solution(mesh):
    n = mesh.shape["modes"]
    return jax.shard_map(
        functools.partial(per_device, n),
        mesh=mesh,
        in_specs=(
            P(("groups", "modes"), None, None),
            P("groups"),
            P("groups"),
            P(("groups", "modes"), None),
            P(("groups", "modes"), None),
            P(("groups", "modes"), None),
            P(("groups", "modes"), None),
        ),
        out_specs=(P(("groups", "modes"), None), P(("groups", "modes"), None)),
        check_vma=False,
    )
```

profile of v0, /device:TPU:5, one launch (start us, length us, event | category | flops | bytes accessed | tf_op | source)
XLA Modules:
  0.0 35.3 jit_solution(6599262630691271704)
XLA Ops:
  0.6 31.5 %posterior_ice.1 = (f32[16,2048]{1,0:T(8,128)}, f32[16,2048]{1,0:T(8,128)}) custom-call(f32[1,128]{1,0:T(1,128)} %bitcast.2, f32[1,128]{1,0:T(1,128)} %bitcast.3, f32[16,2048]{1,0:T(8,128)} %map_hbm.1, f32[16,2048]{1,0:T(8,128)} %bed_hbm.1, f32[16,2048]{1,0:T(8,128)} %smb_hbm.1, f32[16,2048]{1,0:T(8,128)} %h0_hbm.1, bf16[8,256,2048]{2,1,0:T(8,128)(2,1)} %fields_ref.1), custom_call_target="tpu_custom_call" | custom-call | tf_op jit(solution)/shard_map/posterior_ice/pallas_call | solution.py:344
  32.1 1.6 %copy.11 = f32[16,2048]{1,0:T(8,128)} copy(f32[16,2048]{1,0:T(8,128)} %get-tuple-element.4) | data formatting | bytes 262144
  33.7 1.6 %copy.12 = f32[16,2048]{1,0:T(8,128)} copy(f32[16,2048]{1,0:T(8,128)} %get-tuple-element.5) | data formatting | bytes 262144
where the time goes:
time: 35.4 us; the launch traced here: 35.3 us
  Pallas kernels  31.5 us (89%)
  local copies, waits for them, and re-layouts  3.14 us (9%)
  between operations  0.64 us (2%)
    pallas_call x1, Pallas kernels, per_device(): pl.pallas_call(functools.partial(kernel, n), out_shape=(jax.ShapeDtypeStr...  31.5 us
    unnamed x2, local copies, waits for them, and re-layouts  3.14 us

commit v1 on v0

v1 whole, which is shorter than its diff:
```python
import functools

import jax
import jax.numpy as jnp
from jax import lax
from jax.experimental import pallas as pl
from jax.experimental.pallas import tpu as pltpu
from jax.sharding import PartitionSpec as P

STEPS = 8

flow_rate = 0.02
slide_rate = 0.1
diff_cap = 0.5
time_step = 0.4

WIRE = jnp.bfloat16
PAD = 8
LANES = 128
GROUP = 4
F32 = jnp.float32


def flip(x, k):
    bit = 1
    while bit <= k:
        if k & bit:
            x = x + bit - 2 * bit * (x // bit % 2)
        bit *= 2
    return x


def gather_kernel(
    n, H,
    coeff_hbm, eigen_hbm, map_hbm, bed_hbm, smb_hbm, h0_hbm, fields_ref,
    logf_ref, ext_b, ext_e, ext_m, ext_h, ext_s,
    coeff_ref, eigen_ref, map_ref, bed_ref, smb_ref, h0_ref, in_sem,
    mf, p1out, p1own, p1in, s2out, s2in, s3out, s3in,
    st_out, st_in, f_out, f_in,
    mf_sem, p1s, p1r, s2s, s2r, s3s, s3r, hs, hr,
):
    me = lax.axis_index("modes")
    c = me % 2
    a = (me // 2) % 2
    b = me // 4
    B = n // 4
    mode_dev = fields_ref.shape[0]
    rows, cols = map_ref.shape
    cw = cols // H
    ks = list(range(B - 1, -1, -1))
    Q = B * H

    hbm = (coeff_hbm, eigen_hbm, bed_hbm, smb_hbm, h0_hbm, map_hbm)
    own = (coeff_ref, eigen_ref, bed_ref, smb_ref, h0_ref, map_ref)
    takes = [pltpu.make_async_copy(x, y, in_sem.at[i]) for i, (x, y) in enumerate(zip(hbm, own))]
    for take in takes:
        take.start()

    def load(i):
        k, aa, hh, cc = B - 1 - i // (2 * H) % B, 1 - i // (2 * Q), i // 2 % H, 1 - i % 2
        bit, z = 1, b
        while bit < B:
            on = k // bit % 2
            z = z + on * (bit - 2 * bit * (b // bit % 2))
            bit *= 2
        strip = (z * 2 + (a + aa - 2 * a * aa)) * 2 + (c + cc - 2 * c * cc)
        rr = pl.ds(pl.multiple_of(strip * rows, rows), rows)
        cc_ = pl.ds(pl.multiple_of(hh * cw, cw), cw)
        return pltpu.make_async_copy(fields_ref.at[:, rr, cc_], mf.at[i], mf_sem.at[i])

    def go(i, carry):
        load(i).start()
        return carry
    lax.fori_loop(0, n * H, go, 0)

    left, right = lax.rem(me + n - 1, n), lax.rem(me + 1, n)
    core_peer = me + 1 - 2 * c
    y_peer = me + 2 - 4 * a
    barrier = pltpu.get_barrier_semaphore()

    def z_peer(k):
        return (flip(b, k) * 2 + a) * 2 + c

    for peer in [left, right, core_peer, y_peer] + [z_peer(k) for k in range(1, B)]:
        pl.semaphore_signal(barrier, inc=1, device_id={"modes": peer}, device_id_type=pl.DeviceIdType.MESH)

    takes[0].wait()
    takes[1].wait()
    w = coeff_ref[...] / jnp.sqrt(1.0 + eigen_ref[...])
    w = w.astype(jnp.bfloat16).astype(F32)
    lane = lax.broadcasted_iota(jnp.int32, w.shape, 1)
    ws = []
    for j in range(mode_dev):
        picked = jnp.where(lane == me * mode_dev + j, w, 0.0)
        ws.append(jnp.sum(picked, axis=1, keepdims=True))
    for take in takes[2:]:
        take.wait()
    st_out[0] = bed_ref[...].astype(jnp.bfloat16)
    st_out[1] = smb_ref[...].astype(jnp.bfloat16)
    st_out[2] = h0_ref[...].astype(jnp.bfloat16)

    with jax.named_scope("barrier_w"):
        pl.semaphore_wait(barrier, 4 + B - 1)

    def remote(src, dst, ssem, rsem, peer):
        return pltpu.make_async_remote_copy(
            src_ref=src, dst_ref=dst, send_sem=ssem, recv_sem=rsem,
            device_id={"modes": peer}, device_id_type=pl.DeviceIdType.MESH)

    def halo(kind, side):
        src = (st_out, f_out)[kind]
        dst = (st_in, f_in)[kind]
        peer = right if side == 0 else left
        at = kind * 2 + side
        return remote(src, dst.at[side], hs.at[at], hr.at[at], peer)

    has_up, has_down = me > 0, me < n - 1
    at4 = me % 4

    def send_halo(kind, side, ok):
        here = has_down if side == 0 else has_up

        @pl.when(jnp.logical_and(here, ok))
        def _():
            halo(kind, side).start()

    def wait_halo(kind):
        @pl.when(has_down)
        def _():
            halo(kind, 0).wait_send()
            halo(kind, 1).wait_recv()

        @pl.when(has_up)
        def _():
            halo(kind, 1).wait_send()
            halo(kind, 0).wait_recv()

    send_halo(0, 0, at4 != 1)
    send_halo(0, 1, at4 != 2)

    CT = min(512, cw)

    def col_loop(body, width=cw):
        def step(j, carry):
            body(pl.ds(pl.multiple_of(j * CT, CT), CT))
            return carry
        lax.fori_loop(0, width // CT, step, 0)

    def partial(i, out):
        load(i).wait()

        def body(cs):
            tot = None
            for j in range(mode_dev):
                term = mf[i, j, :, cs].astype(F32) * ws[j]
                tot = term if tot is None else tot + term
            out[:, cs] = tot
        col_loop(body)

    def s1copy(m):
        return remote(p1out.at[m], p1in.at[m], p1s.at[m], p1r.at[m], core_peer)

    def stage1(m):
        with jax.named_scope("s1_%d" % m):
            partial(2 * m, p1out.at[m])
            s1copy(m).start()
            partial(2 * m + 1, p1own.at[m])

    def s2copy(q):
        return remote(s2out.at[q], s2in.at[q], s2s.at[q], s2r.at[q], y_peer)

    def stage2(q):
        with jax.named_scope("s2_%d" % q):
            s1copy(q).wait_recv()

            def body(cs):
                s2out[q, :, cs] = (p1own[q, :, cs] + p1in[q, :, cs]).astype(WIRE)
            col_loop(body)
            s2copy(q).start()

    def s3copy(q):
        return remote(s3out.at[q], s3in.at[q], s3s.at[q], s3r.at[q], z_peer(ks[q // H]))

    def stage3(q):
        with jax.named_scope("s3_%d" % q):
            m = Q + q
            s1copy(m).wait_recv()
            s2copy(q).wait_recv()
            k, hh = ks[q // H], q % H

            def body(cs):
                tot = p1own[m, :, cs] + p1in[m, :, cs] + s2in[q, :, cs].astype(F32)
                if k:
                    s3out[q, :, cs] = tot.astype(WIRE)
                else:
                    p1own[m, :, cs] = tot
            col_loop(body)
            if k:
                s3copy(q).start()

    tiles = cols // LANES
    top, mid, low = pl.ds(PAD, rows), pl.ds(PAD + rows, rows), pl.ds(PAD + 2 * rows, rows)
    whole = 3 * rows + 2 * PAD

    def clear(ref, where, size):
        for j in range(tiles):
            ref[j + 1, where, :] = jnp.zeros((size, LANES), F32)

    def lanes(j):
        return slice(j * LANES, (j + 1) * LANES)

    stage1(0)
    for q in range(1, Q):
        stage1(q)
        stage2(q - 1)
    stage1(Q)
    stage2(Q - 1)
    send_halo(0, 0, at4 == 1)
    send_halo(0, 1, at4 == 2)
    for q in range(1, Q):
        stage1(Q + q)

    clear(ext_s, pl.ds(0, PAD), PAD)
    clear(ext_s, pl.ds(PAD + 3 * rows, PAD), PAD)
    for j in (0, tiles + 1):
        ext_s[j] = jnp.zeros((whole, LANES), F32)
    for j in range(tiles):
        bb, hh = bed_ref[:, lanes(j)], h0_ref[:, lanes(j)]
        ext_b[j + 1, mid, :] = bb
        ext_m[j + 1, mid, :] = time_step * smb_ref[:, lanes(j)]
        ext_h[j + 1, mid, :] = hh
        ext_s[j + 1, mid, :] = bb + hh

    for q in range(Q):
        stage3(q)
    with jax.named_scope("s3wait"):
        for q in range(Q - H):
            s3copy(q).wait_recv()

    def finish(hh):
        off = hh * cw

        def body(cs):
            tot = p1own[2 * Q - H + hh, :, cs]
            for q in range(hh, Q - H, H):
                tot = tot + s3in[q, :, cs].astype(F32)
            return tot

        def step(j, carry):
            cs = pl.ds(pl.multiple_of(j * CT, CT), CT)
            out = pl.ds(pl.multiple_of(off + j * CT, CT), CT)
            tot = body(cs) + map_ref[:, out]
            logf_ref[:, out] = tot
            f_out[:, out] = tot.astype(jnp.bfloat16)
            return carry
        lax.fori_loop(0, cw // CT, step, 0)
    for hh in range(H):
        finish(hh)
    send_halo(1, 0, True)
    send_halo(1, 1, True)

    for j in range(tiles):
        ext_e[j + 1, mid, :] = slide_rate * jnp.exp(-logf_ref[:, lanes(j)])
    with jax.named_scope("halo0"):
        wait_halo(0)

    def fill(side, where, present):
        @pl.when(present)
        def _():
            for j in range(tiles):
                bb = st_in[side, 0, :, lanes(j)].astype(F32)
                hh = st_in[side, 2, :, lanes(j)].astype(F32)
                ext_b[j + 1, where, :] = bb
                ext_m[j + 1, where, :] = time_step * st_in[side, 1, :, lanes(j)].astype(F32)
                ext_h[j + 1, where, :] = hh
                ext_s[j + 1, where, :] = bb + hh

        @pl.when(jnp.logical_not(present))
        def _():
            clear(ext_s, where, rows)
    fill(0, top, has_up)
    fill(1, low, has_down)
    for m in range(2 * Q):
        s1copy(m).wait_send()
    for q in range(Q):
        s2copy(q).wait_send()
        if ks[q // H]:
            s3copy(q).wait_send()
    with jax.named_scope("halo1"):
        wait_halo(1)

    def fill_e(side, where, present):
        @pl.when(present)
        def _():
            for j in range(tiles):
                ext_e[j + 1, where, :] = slide_rate * jnp.exp(-f_in[side, :, lanes(j)].astype(F32))
    fill_e(0, top, has_up)
    fill_e(1, low, has_down)


def step_kernel(n, rows, logf_ref, ext_b, ext_e, ext_m, in_h, in_s, logf_hbm, final_hbm, final_ref, out_sem, ext_h, ext_d, ext_g, ext_s0, ext_s1):
    me = lax.axis_index("modes")
    has_up, has_down = me > 0, me < n - 1
    tiles = ext_b.shape[0] - 2
    whole = 3 * rows + 2 * PAD
    top, mid, low = pl.ds(PAD, rows), pl.ds(PAD + rows, rows), pl.ds(PAD + 2 * rows, rows)
    gives = [pltpu.make_async_copy(x, y, out_sem.at[i]) for i, (x, y) in enumerate(((logf_ref, logf_hbm), (final_ref, final_hbm)))]
    gives[0].start()

    def lanes(j):
        return slice(j * LANES, (j + 1) * LANES)

    def clear(ref, where, size):
        for j in range(tiles):
            ref[j + 1, where, :] = jnp.zeros((size, LANES), F32)

    for ref in (ext_s0, ext_s1, ext_d):
        clear(ref, pl.ds(0, PAD), PAD)
        clear(ref, pl.ds(PAD + 3 * rows, PAD), PAD)
        for j in (0, tiles + 1):
            ref[j] = jnp.zeros((whole, LANES), F32)
    ext_g[0] = jnp.zeros((whole, LANES), F32)
    for where, present in ((top, has_up), (low, has_down)):
        @pl.when(jnp.logical_not(present))
        def _():
            for ref in (ext_s0, ext_s1, ext_d):
                clear(ref, where, rows)

    margin = rows - 2 * STEPS

    def sweep(first, last, body):
        for lo, hi, present in ((0, rows, has_up), (rows, 2 * rows, None), (2 * rows, 3 * rows, has_down)):
            lo, hi = max(lo, first // 8 * 8), min(hi, -(-last // 8) * 8)
            if lo >= hi:
                continue
            if present is None:
                body(PAD + lo, hi - lo)
            else:
                pl.when(present)(functools.partial(body, PAD + lo, hi - lo))

    for t in range(1, STEPS + 1):
        s_ref, s_new = (ext_s0, ext_s1) if t % 2 else (ext_s1, ext_s0)
        s_ref, h_ref = (in_s, in_h) if t == 1 else (s_ref, ext_h)
        lo_h = margin + 2 * t

        lane = lax.broadcasted_iota(jnp.int32, (1, 8, LANES), 2)
        first_lane, last_lane = lane == 0, lane == LANES - 1

        def d_rows(r, size):
            for at in range(r, r + size, 8):
                here, up, down = (slice(at + o, at + o + 8) for o in (0, -1, 1))
                for j in range(1, tiles + 1, GROUP):
                    now, later, sooner = (slice(j + o, j + o + GROUP) for o in (0, 1, -1))
                    s = s_ref[now, here, :]
                    right = pltpu.roll(jnp.where(first_lane, s_ref[later, here, :], s), LANES - 1, 2)
                    left_ = pltpu.roll(jnp.where(last_lane, s_ref[sooner, here, :], s), 1, 2)
                    gx = s_ref[now, down, :] - s_ref[now, up, :]
                    gy = right - left_
                    h = h_ref[now, here, :]
                    sq = h * h
                    d = sq * ((0.25 * flow_rate) * (sq * h) * (gx * gx + gy * gy) + ext_e[now, here, :])
                    ext_d[now, here, :] = jnp.minimum(d, diff_cap)
                    ext_g[now, here, :] = right - s

        def h_rows(r, size):
            for at in range(r, r + size, 8):
                here, up, down = (slice(at + o, at + o + 8) for o in (0, -1, 1))
                edge = pltpu.roll(ext_d[1:2, here, :] * s_ref[1:2, here, :], LANES - 1, 2)
                for j in range(1, tiles + 1, GROUP):
                    now, later = (slice(j + o, j + o + GROUP) for o in (0, 1))
                    s, d = s_ref[now, here, :], ext_d[now, here, :]
                    right = pltpu.roll(jnp.where(first_lane, ext_d[later, here, :], d), LANES - 1, 2)
                    flux = (right + d) * ext_g[now, here, :]
                    sooner = jnp.concatenate([edge, flux[:-1]], axis=0)
                    edge = flux[-1:]
                    div = (ext_d[now, down, :] + d) * (s_ref[now, down, :] - s)
                    div += (ext_d[now, up, :] + d) * (s_ref[now, up, :] - s)
                    div += flux - pltpu.roll(jnp.where(last_lane, sooner, flux), 1, 2)
                    h = jnp.maximum(h_ref[now, here, :] + ((0.5 * time_step) * div + ext_m[now, here, :]), 0.0)
                    ext_h[now, here, :] = h
                    if t < STEPS:
                        s_new[now, here, :] = ext_b[now, here, :] + h

        with jax.named_scope("step%d_d" % t):
            sweep(lo_h - 1, 3 * rows - lo_h + 1, d_rows)
        with jax.named_scope("step%d_h" % t):
            sweep(lo_h, 3 * rows - lo_h, h_rows)

    for j in range(tiles):
        final_ref[:, lanes(j)] = ext_h[j + 1, mid, :]
    gives[1].start()
    gives[0].wait()
    gives[1].wait()


def per_device(n, mode_fields, coeff, eigen, map_friction, bed, smb, thickness):
    rows, cols = map_friction.shape
    mode_dev = mode_fields.shape[0]
    B = n // 4
    H = 2 if n <= 16 else 1
    Q = B * H
    modes = coeff.shape[0]
    anywhere = pl.BlockSpec(memory_space=pl.ANY)
    vmem = pl.BlockSpec(memory_space=pltpu.VMEM)
    strip = (rows, cols)
    part = (rows, cols // H)
    ext = (cols // LANES + 2, 3 * rows + 2 * PAD, LANES)
    bf = jnp.bfloat16
    dma = pltpu.SemaphoreType.DMA
    outs = pl.pallas_call(
        functools.partial(gather_kernel, n, H),
        out_shape=(pltpu.VMEM(strip, F32),) + (pltpu.VMEM(ext, F32),) * 5,
        in_specs=[anywhere] * 7,
        out_specs=(vmem,) * 6,
        scratch_shapes=[
            pltpu.VMEM((1, modes), F32),
            pltpu.VMEM((1, modes), F32),
        ] + [pltpu.VMEM(strip, F32)] * 4 + [
            dma((6,)),
            pltpu.VMEM((n * H, mode_dev) + part, bf),
            pltpu.VMEM((2 * Q,) + part, F32),
            pltpu.VMEM((2 * Q,) + part, F32),
            pltpu.VMEM((2 * Q,) + part, F32),
            pltpu.VMEM((Q,) + part, WIRE),
            pltpu.VMEM((Q,) + part, WIRE),
            pltpu.VMEM((Q,) + part, WIRE),
            pltpu.VMEM((Q,) + part, WIRE),
            pltpu.VMEM((3,) + strip, bf),
            pltpu.VMEM((2, 3) + strip, bf),
            pltpu.VMEM(strip, bf),
            pltpu.VMEM((2,) + strip, bf),
            dma((n * H,)), dma((2 * Q,)), dma((2 * Q,)), dma((Q,)), dma((Q,)), dma((Q,)), dma((Q,)), dma((4,)), dma((4,)),
        ],
        compiler_params=pltpu.CompilerParams(collective_id=0, has_side_effects=True, vmem_limit_bytes=52 * 2**20),
        name="posterior_gather",
    )(coeff.reshape(1, modes), eigen.reshape(1, modes), map_friction, bed, smb, thickness, mode_fields)
    return pl.pallas_call(
        functools.partial(step_kernel, n, rows),
        out_shape=(jax.ShapeDtypeStruct(strip, F32),) * 2,
        in_specs=[vmem] * 6,
        out_specs=(anywhere, anywhere),
        scratch_shapes=[pltpu.VMEM(strip, F32), dma((2,))] + [pltpu.VMEM(ext, F32)] * 5,
        compiler_params=pltpu.CompilerParams(vmem_limit_bytes=16 * 2**20),
        name="ice_steps",
    )(*outs)


def solution(mesh):
    n = mesh.shape["modes"]
    return jax.shard_map(
        functools.partial(per_device, n),
        mesh=mesh,
        in_specs=(
            P(("groups", "modes"), None, None),
            P("groups"),
            P("groups"),
            P(("groups", "modes"), None),
            P(("groups", "modes"), None),
            P(("groups", "modes"), None),
            P(("groups", "modes"), None),
        ),
        out_specs=(P(("groups", "modes"), None), P(("groups", "modes"), None)),
        check_vma=False,
    )
```

time: 35.4 us -> 33.6 us (0.949)
  the two profiles are of different devices: /device:TPU:5 before, /device:TPU:1 now
where the time goes in v1:
time: 33.6 us; the launch traced here: 33.5 us
  Pallas kernels  32.8 us (98%)
  between operations  0.64 us (2%)
    pallas_call x1, Pallas kernels, per_device(): pl.pallas_call(functools.partial(gather_kernel, n, H), out_shape=(pltpu.V...  23.8 us
    pallas_call x1, Pallas kernels, per_device(): pl.pallas_call(functools.partial(step_kernel, n, rows), out_shape=(jax.Sh...  9.07 us

profile of v1, /device:TPU:1, one launch (start us, length us, event | category | flops | bytes accessed | tf_op | source)
XLA Modules:
  0.0 33.5 jit_solution(1679992856811776753)
XLA Ops:
  0.6 23.8 %posterior_gather.1 = (f32[16,2048]{1,0:T(8,128)S(1)}, f32[18,64,128]{2,1,0:T(8,128)S(1)}, f32[18,64,128]{2,1,0:T(8,128)S(1)}, f32[18,64,128]{2,1,0:T(8,128)S(1)...) custom-call(f32[1,128]{1,0:T(1,128)} %bitcast.2, f32[1,128]{1,0:T(1,128)} %bitcast.3, f32[16,2048]{1,0:T(8,128)} %map_hbm.1, ...), custom_call_target="tpu_custom_call" | custom-call | tf_op jit(solution)/shard_map/posterior_gather/pallas_call | solution.py:410
  24.4 9.1 %ice_steps.1 = (f32[16,2048]{1,0:T(8,128)}, f32[16,2048]{1,0:T(8,128)}) custom-call(f32[16,2048]{1,0:T(8,128)S(1)} %get-tuple-element.8.logf_ref, f32[18,64,128]{2,1,0:T(8,128)S(1)} %get-tuple-element.9.ext_b, f32[18,64,128]{2,1,0:T(8,128)S(1)} %get-tuple-element.10.ext_e, f32[18,64,128]{2,1,0:T(8,128)S(1)} %get-tuple-element.11.ext_m, ...), custom_call_target="tpu_custom_call" | custom-call | tf_op jit(solution)/shard_map/ice_steps/pallas_call | solution.py:437

commit v2 on v1

--- a/solution.py
+++ b/solution.py
@@ -81,8 +81,15 @@
     def z_peer(k):
         return (flip(b, k) * 2 + a) * 2 + c
 
-    for peer in [left, right, core_peer, y_peer] + [z_peer(k) for k in range(1, B)]:
+    has_up, has_down = me > 0, me < n - 1
+
+    def greet(peer):
         pl.semaphore_signal(barrier, inc=1, device_id={"modes": peer}, device_id_type=pl.DeviceIdType.MESH)
+
+    for peer in [core_peer, y_peer] + [z_peer(k) for k in range(1, B)]:
+        greet(peer)
+    pl.when(has_up)(lambda: greet(left))
+    pl.when(has_down)(lambda: greet(right))
 
     takes[0].wait()
     takes[1].wait()
@@ -93,14 +100,6 @@
     for j in range(mode_dev):
         picked = jnp.where(lane == me * mode_dev + j, w, 0.0)
         ws.append(jnp.sum(picked, axis=1, keepdims=True))
-    for take in takes[2:]:
-        take.wait()
-    st_out[0] = bed_ref[...].astype(jnp.bfloat16)
-    st_out[1] = smb_ref[...].astype(jnp.bfloat16)
-    st_out[2] = h0_ref[...].astype(jnp.bfloat16)
-
-    with jax.named_scope("barrier_w"):
-        pl.semaphore_wait(barrier, 4 + B - 1)
 
     def remote(src, dst, ssem, rsem, peer):
         return pltpu.make_async_remote_copy(
@@ -114,7 +113,6 @@
         at = kind * 2 + side
         return remote(src, dst.at[side], hs.at[at], hr.at[at], peer)
 
-    has_up, has_down = me > 0, me < n - 1
     at4 = me % 4
 
     def send_halo(kind, side, ok):
@@ -134,9 +132,6 @@
         def _():
             halo(kind, 1).wait_send()
             halo(kind, 0).wait_recv()
-
-    send_halo(0, 0, at4 != 1)
-    send_halo(0, 1, at4 != 2)
 
     CT = min(512, cw)
 
@@ -165,6 +160,10 @@
             partial(2 * m, p1out.at[m])
             s1copy(m).start()
             partial(2 * m + 1, p1own.at[m])
+
+    def meet():
+        with jax.named_scope("barrier_w"):
+            pl.semaphore_wait(barrier, B + 1 + (me + n - 1) // n + (2 * n - 2 - me) // n)
 
     def s2copy(q):
         return remote(s2out.at[q], s2in.at[q], s2s.at[q], s2r.at[q], y_peer)
@@ -209,16 +208,27 @@
     def lanes(j):
         return slice(j * LANES, (j + 1) * LANES)
 
-    stage1(0)
-    for q in range(1, Q):
-        stage1(q)
-        stage2(q - 1)
-    stage1(Q)
-    stage2(Q - 1)
+    partial(0, p1out.at[0])
+    meet()
+    s1copy(0).start()
+    partial(1, p1own.at[0])
+    lead = 4
+    for m in range(1, lead):
+        stage1(m)
+    for take in takes[2:]:
+        take.wait()
+    st_out[0] = bed_ref[...].astype(jnp.bfloat16)
+    st_out[1] = smb_ref[...].astype(jnp.bfloat16)
+    st_out[2] = h0_ref[...].astype(jnp.bfloat16)
+    send_halo(0, 0, c == 0)
+    send_halo(0, 1, c == 1)
+    for q in range(Q):
+        stage1(q + lead)
+        stage2(q)
     send_halo(0, 0, at4 == 1)
     send_halo(0, 1, at4 == 2)
-    for q in range(1, Q):
-        stage1(Q + q)
+    for m in range(Q + lead, 2 * Q):
+        stage1(m)
 
     clear(ext_s, pl.ds(0, PAD), PAD)
     clear(ext_s, pl.ds(PAD + 3 * rows, PAD), PAD)
@@ -233,6 +243,8 @@
 
     for q in range(Q):
         stage3(q)
+    send_halo(0, 0, at4 == 3)
+    send_halo(0, 1, at4 == 0)
     with jax.named_scope("s3wait"):
         for q in range(Q - H):
             s3copy(q).wait_recv()

time: 33.6 us -> 31.5 us (0.938)
  Pallas kernels: 32.8 us -> 30.7 us
    pallas_call x1, Pallas kernels: 23.8 us -> 21.7 us  [per_device(): pl.pallas_call(functools.partial(gather_kernel, n, H), out_shape=(pltpu.V...]
where the time goes in v2:
time: 31.5 us; the launch traced here: 31.4 us
  Pallas kernels  30.7 us (97%)
  between operations  0.64 us (2%)
    pallas_call x1, Pallas kernels, per_device(): pl.pallas_call(functools.partial(gather_kernel, n, H), out_shape=(pltpu.V...  21.7 us
    pallas_call x1, Pallas kernels, per_device(): pl.pallas_call(functools.partial(step_kernel, n, rows), out_shape=(jax.Sh...  9.07 us

profile of v2, /device:TPU:1, one launch (start us, length us, event | category | flops | bytes accessed | tf_op | source)
XLA Modules:
  0.0 31.4 jit_solution(15783863680277880338)
XLA Ops:
  0.6 21.7 %posterior_gather.1 = (f32[16,2048]{1,0:T(8,128)S(1)}, f32[18,64,128]{2,1,0:T(8,128)S(1)}, f32[18,64,128]{2,1,0:T(8,128)S(1)}, f32[18,64,128]{2,1,0:T(8,128)S(1)...) custom-call(f32[1,128]{1,0:T(1,128)} %bitcast.2, f32[1,128]{1,0:T(1,128)} %bitcast.3, f32[16,2048]{1,0:T(8,128)} %map_hbm.1, ...), custom_call_target="tpu_custom_call" | custom-call | tf_op jit(solution)/shard_map/posterior_gather/pallas_call | solution.py:422
  22.3 9.1 %ice_steps.1 = (f32[16,2048]{1,0:T(8,128)}, f32[16,2048]{1,0:T(8,128)}) custom-call(f32[16,2048]{1,0:T(8,128)S(1)} %get-tuple-element.8.logf_ref, f32[18,64,128]{2,1,0:T(8,128)S(1)} %get-tuple-element.9.ext_b, f32[18,64,128]{2,1,0:T(8,128)S(1)} %get-tuple-element.10.ext_e, f32[18,64,128]{2,1,0:T(8,128)S(1)} %get-tuple-element.11.ext_m, ...), custom_call_target="tpu_custom_call" | custom-call | tf_op jit(solution)/shard_map/ice_steps/pallas_call | solution.py:449

commit v3 on v2

v3 whole, which is shorter than its diff:
```python
import functools

import jax
import jax.numpy as jnp
from jax import lax
from jax.experimental import pallas as pl
from jax.experimental.pallas import tpu as pltpu
from jax.sharding import PartitionSpec as P

STEPS = 8

flow_rate = 0.02
slide_rate = 0.1
diff_cap = 0.5
time_step = 0.4

WIRE = jnp.bfloat16
PAD = 8
LANES = 128
F32 = jnp.float32
SUB = 8

damp = 0.5 * time_step
unit = (damp * 0.25 * flow_rate) ** (1.0 / 7.0)
slide = damp * slide_rate / unit**2
dry = -1e30


def flip(x, k):
    bit = 1
    while bit <= k:
        if k & bit:
            x = x + bit - 2 * bit * (x // bit % 2)
        bit *= 2
    return x


def gather_kernel(
    n, H,
    coeff_hbm, eigen_hbm, map_hbm, bed_hbm, smb_hbm, h0_hbm, fields_ref,
    logf_ref, pl_b, pl_e, pl_m, pl_h,
    coeff_ref, eigen_ref, map_ref, bed_ref, smb_ref, h0_ref, in_sem,
    mf, p1out, p1own, p1in, s2out, s2in, s3out, s3in,
    st_out, st_in, st_via, f_out, f_in, ext_b, ext_e, ext_m, ext_h,
    mf_sem, p1s, p1r, s2s, s2r, s3s, s3r, hs, hr, via_s, via_r,
):
    me = lax.axis_index("modes")
    c = me % 2
    a = (me // 2) % 2
    b = me // 4
    B = n // 4
    mode_dev = fields_ref.shape[0]
    rows, cols = map_ref.shape
    cw = cols // H
    ks = list(range(B - 1, -1, -1))
    Q = B * H

    hbm = (coeff_hbm, eigen_hbm, bed_hbm, smb_hbm, h0_hbm, map_hbm)
    own = (coeff_ref, eigen_ref, bed_ref, smb_ref, h0_ref, map_ref)
    takes = [pltpu.make_async_copy(x, y, in_sem.at[i]) for i, (x, y) in enumerate(zip(hbm, own))]
    for take in takes:
        take.start()

    def load(i):
        k, aa, hh, cc = B - 1 - i // (2 * H) % B, 1 - i // (2 * Q), i // 2 % H, 1 - i % 2
        bit, z = 1, b
        while bit < B:
            on = k // bit % 2
            z = z + on * (bit - 2 * bit * (b // bit % 2))
            bit *= 2
        strip = (z * 2 + (a + aa - 2 * a * aa)) * 2 + (c + cc - 2 * c * cc)
        rr = pl.ds(pl.multiple_of(strip * rows, rows), rows)
        cc_ = pl.ds(pl.multiple_of(hh * cw, cw), cw)
        return pltpu.make_async_copy(fields_ref.at[:, rr, cc_], mf.at[i], mf_sem.at[i])

    def go(i, carry):
        load(i).start()
        return carry
    lax.fori_loop(0, n * H, go, 0)

    left, right = lax.rem(me + n - 1, n), lax.rem(me + 1, n)
    core_peer = me + 1 - 2 * c
    y_peer = me + 2 - 4 * a
    barrier = pltpu.get_barrier_semaphore()

    def z_peer(k):
        return (flip(b, k) * 2 + a) * 2 + c

    has_up, has_down = me > 0, me < n - 1
    at4 = me % 4

    def greet(peer):
        pl.semaphore_signal(barrier, inc=1, device_id={"modes": peer}, device_id_type=pl.DeviceIdType.MESH)

    for peer in [core_peer, y_peer] + [z_peer(k) for k in range(1, B)]:
        greet(peer)
    pl.when(has_up)(lambda: greet(left))
    pl.when(has_down)(lambda: greet(right))
    pl.when(at4 == 0)(lambda: greet(me + 3))
    pl.when(at4 == 3)(lambda: greet(me - 3))

    takes[0].wait()
    takes[1].wait()
    w = coeff_ref[...] / jnp.sqrt(1.0 + eigen_ref[...])
    w = w.astype(jnp.bfloat16).astype(F32)
    lane = lax.broadcasted_iota(jnp.int32, w.shape, 1)
    ws = []
    for j in range(mode_dev):
        picked = jnp.where(lane == me * mode_dev + j, w, 0.0)
        ws.append(jnp.sum(picked, axis=1, keepdims=True))

    def remote(src, dst, ssem, rsem, peer):
        return pltpu.make_async_remote_copy(
            src_ref=src, dst_ref=dst, send_sem=ssem, recv_sem=rsem,
            device_id={"modes": peer}, device_id_type=pl.DeviceIdType.MESH)

    def halo(side):
        return remote(st_out, st_in.at[side], hs.at[side], hr.at[side], right if side == 0 else left)

    def f_halo(hh, side):
        at = 2 + hh * 2 + side
        return remote(f_out.at[hh], f_in.at[side, hh], hs.at[at], hr.at[at], right if side == 0 else left)

    def send_halo(side, ok):
        here = has_down if side == 0 else has_up

        @pl.when(jnp.logical_and(here, ok))
        def _():
            halo(side).start()

    def hop(side):
        return remote(st_out, st_via, hs.at[side], via_r.at[0], me + 4 - 8 * side)

    def forward(side):
        return remote(st_via, st_in.at[side], via_s.at[0], hr.at[side], me - 3 + 6 * side)

    lower, upper = me >= 4, me < n - 4
    seats = [jnp.logical_and(at4 == 3, upper), jnp.logical_and(at4 == 0, lower)]
    vias = [jnp.logical_and(at4 == 3, lower), jnp.logical_and(at4 == 0, upper)]

    def swap(do):
        for side in (0, 1):
            for ok, what in zip((seats[side], vias[side]), do):
                if what:
                    pl.when(ok)(functools.partial(what, side))

    def wait_halo():
        @pl.when(has_down)
        def _():
            halo(0).wait_send()
            halo(1).wait_recv()

        @pl.when(has_up)
        def _():
            halo(1).wait_send()
            halo(0).wait_recv()

    def wait_f():
        for hh in range(H):
            @pl.when(has_down)
            def _():
                f_halo(hh, 0).wait_send()
                f_halo(hh, 1).wait_recv()

            @pl.when(has_up)
            def _():
                f_halo(hh, 1).wait_send()
                f_halo(hh, 0).wait_recv()

    CT = min(512, cw)

    def col_loop(body, width=cw):
        def step(j, carry):
            body(pl.ds(pl.multiple_of(j * CT, CT), CT))
            return carry
        lax.fori_loop(0, width // CT, step, 0)

    def partial(i, out):
        load(i).wait()

        def body(cs):
            tot = None
            for j in range(mode_dev):
                term = mf[i, j, :, cs].astype(F32) * ws[j]
                tot = term if tot is None else tot + term
            out[:, cs] = tot
        col_loop(body)

    def s1copy(m):
        return remote(p1out.at[m], p1in.at[m], p1s.at[m], p1r.at[m], core_peer)

    def stage1(m):
        with jax.named_scope("s1_%d" % m):
            partial(2 * m, p1out.at[m])
            s1copy(m).start()
            partial(2 * m + 1, p1own.at[m])

    def meet():
        with jax.named_scope("barrier_w"):
            pl.semaphore_wait(barrier, B + 1 + (me + n - 1) // n + (2 * n - 2 - me) // n + 1 - (at4 + 1) // 2 % 2)

    def s2copy(q):
        return remote(s2out.at[q], s2in.at[q], s2s.at[q], s2r.at[q], y_peer)

    def stage2(q):
        with jax.named_scope("s2_%d" % q):
            s1copy(q).wait_recv()

            def body(cs):
                s2out[q, :, cs] = (p1own[q, :, cs] + p1in[q, :, cs]).astype(WIRE)
            col_loop(body)
            s2copy(q).start()

    def s3copy(q):
        return remote(s3out.at[q], s3in.at[q], s3s.at[q], s3r.at[q], z_peer(ks[q // H]))

    def stage3(q):
        with jax.named_scope("s3_%d" % q):
            m = Q + q
            s1copy(m).wait_recv()
            s2copy(q).wait_recv()
            k, hh = ks[q // H], q % H

            def body(cs):
                tot = p1own[m, :, cs] + p1in[m, :, cs] + s2in[q, :, cs].astype(F32)
                if k:
                    s3out[q, :, cs] = tot.astype(WIRE)
                else:
                    p1own[m, :, cs] = tot
            col_loop(body)
            if k:
                s3copy(q).start()

    tiles = cols // LANES
    top, mid, low = pl.ds(0, rows), pl.ds(rows, rows), pl.ds(2 * rows, rows)

    def lanes(j):
        return slice(j * LANES, (j + 1) * LANES)

    def turn(ext, planes):
        G = planes.shape[0]
        for g in range(G):
            block = jnp.concatenate([ext[j, pl.ds(g, SUB, stride=G), :] for j in range(tiles)], axis=0)
            planes[g] = block.T

    partial(0, p1out.at[0])
    meet()
    s1copy(0).start()
    partial(1, p1own.at[0])
    lead = 4
    for m in range(1, lead):
        stage1(m)
    for take in takes[2:]:
        take.wait()
    st_out[0] = bed_ref[...].astype(jnp.bfloat16)
    st_out[1] = smb_ref[...].astype(jnp.bfloat16)
    st_out[2] = h0_ref[...].astype(jnp.bfloat16)
    send_halo(0, c == 0)
    send_halo(1, c == 1)
    swap((lambda side: hop(side).start(), None))
    for q in range(Q):
        stage1(q + lead)
        stage2(q)
    send_halo(0, at4 == 1)
    send_halo(1, at4 == 2)
    for m in range(Q + lead, 2 * Q):
        stage1(m)

    for j in range(tiles):
        ext_b[j, mid, :] = unit * bed_ref[:, lanes(j)]
        ext_m[j, mid, :] = (unit * time_step) * smb_ref[:, lanes(j)]
        ext_h[j, mid, :] = unit * h0_ref[:, lanes(j)]

    def pass_on(side):
        hop(side).wait_recv()
        forward(side).start()

    for q in range(Q):
        stage3(q)
        if q == min(1, Q - 1):
            with jax.named_scope("relay"):
                swap((None, pass_on))

    def finish(hh):
        off = hh * cw

        def body(cs):
            tot = p1own[2 * Q - H + hh, :, cs]
            for q in range(hh, Q - H, H):
                tot = tot + s3in[q, :, cs].astype(F32)
            return tot

        def step(j, carry):
            cs = pl.ds(pl.multiple_of(j * CT, CT), CT)
            out = pl.ds(pl.multiple_of(off + j * CT, CT), CT)
            tot = body(cs) + map_ref[:, out]
            logf_ref[:, out] = tot
            f_out[hh, :, cs] = tot.astype(jnp.bfloat16)
            return carry
        lax.fori_loop(0, cw // CT, step, 0)
    for hh in range(H):
        with jax.named_scope("s3wait%d" % hh):
            for q in range(hh, Q - H, H):
                s3copy(q).wait_recv()
        finish(hh)

        @pl.when(has_down)
        def _():
            f_halo(hh, 0).start()

        @pl.when(has_up)
        def _():
            f_halo(hh, 1).start()

    for j in range(tiles):
        ext_e[j, mid, :] = slide * jnp.exp(-logf_ref[:, lanes(j)])
    with jax.named_scope("halo0"):
        wait_halo()

    def fill(side, where, present):
        @pl.when(present)
        def _():
            for j in range(tiles):
                ext_b[j, where, :] = unit * st_in[side, 0, :, lanes(j)].astype(F32)
                ext_m[j, where, :] = (unit * time_step) * st_in[side, 1, :, lanes(j)].astype(F32)
                ext_h[j, where, :] = unit * st_in[side, 2, :, lanes(j)].astype(F32)

        @pl.when(jnp.logical_not(present))
        def _():
            for j in range(tiles):
                ext_b[j, where, :] = jnp.zeros((rows, LANES), F32)
                ext_m[j, where, :] = jnp.full((rows, LANES), dry, F32)
                ext_h[j, where, :] = jnp.zeros((rows, LANES), F32)
    fill(0, top, has_up)
    fill(1, low, has_down)
    with jax.named_scope("turn3"):
        turn(ext_b, pl_b)
        turn(ext_m, pl_m)
        turn(ext_h, pl_h)
    swap((None, lambda side: forward(side).wait_send()))
    for m in range(2 * Q):
        s1copy(m).wait_send()
    for q in range(Q):
        s2copy(q).wait_send()
        if ks[q // H]:
            s3copy(q).wait_send()
    with jax.named_scope("halo1"):
        wait_f()

    def fill_e(side, where, present):
        @pl.when(present)
        def _():
            for j in range(tiles):
                ext_e[j, where, :] = slide * jnp.exp(-f_in[side, j * LANES // cw, :, lanes(j % (cw // LANES))].astype(F32))

        @pl.when(jnp.logical_not(present))
        def _():
            for j in range(tiles):
                ext_e[j, where, :] = jnp.zeros((rows, LANES), F32)
    fill_e(0, top, has_up)
    fill_e(1, low, has_down)
    with jax.named_scope("turn_e"):
        turn(ext_e, pl_e)


def step_kernel(logf_ref, b_ref, e_ref, m_ref, h0_ref, logf_hbm, final_hbm, final_ref, out_sem, h_ref, a_ref, f_ref, d_ref, s0_ref, s1_ref, fin):
    rows, cols = final_ref.shape
    G, span = h_ref.shape[0], h_ref.shape[1]
    tiles = cols // LANES
    gives = [pltpu.make_async_copy(x, y, out_sem.at[i]) for i, (x, y) in enumerate(((logf_ref, logf_hbm), (final_ref, final_hbm)))]
    gives[0].start()

    lane = lax.broadcasted_iota(jnp.int32, (1, LANES), 1)
    inner, outer = lane >= SUB, lane < LANES - SUB

    def before(row):
        return jnp.where(inner, pltpu.roll(row, SUB, 1), 0.0)

    def after(row):
        return jnp.where(outer, pltpu.roll(row, LANES - SUB, 1), 0.0)

    def row(ref, g, i):
        return ref[g, PAD + i:PAD + i + 1, :]

    def at(i):
        return slice(PAD + i, PAD + i + SUB)

    def put(ref, g, i, x):
        ref[g + 1, at(i), :] = x
        if g == G - 1:
            ref[0, at(i), :] = pltpu.roll(x, 1, 1)
        if g == 0:
            ref[G + 1, at(i), :] = pltpu.roll(x, LANES - 1, 1)

    def wrap(ref, g):
        ref[g + 1, PAD - 1:PAD, :] = before(row(ref, g + 1, span - 1))
        ref[g + 1, PAD + span:PAD + span + 1, :] = after(row(ref, g + 1, 0))

    for i in range(0, span, SUB):
        for g in range(G):
            h = h0_ref[g, i:i + SUB, :]
            h_ref[g, i:i + SUB, :] = h
            put(s0_ref, g, i, b_ref[g, i:i + SUB, :] + h)
    for g in range(G):
        wrap(s0_ref, g)

    def step(s_ref, s_new):
        for i in range(0, span, SUB):
            here = slice(i, i + SUB)
            up, s = s_ref[0, at(i), :], s_ref[1, at(i), :]
            for g in range(G):
                down = s_ref[g + 2, at(i), :]
                right = s_ref[g + 1, at(i + 1), :]
                gx = down - up
                gy = right - s_ref[g + 1, at(i - 1), :]
                h = h_ref[g, here, :]
                sq = h * h
                d = sq * ((sq * h) * (gx * gx + gy * gy) + e_ref[g, here, :])
                put(d_ref, g, i, jnp.minimum(d, damp * diff_cap))
                a_ref[g, here, :] = right - s
                up, s = s, down
        for g in range(G):
            wrap(d_ref, g)
            first = row(d_ref, g + 1, 0) + row(d_ref, g + 1, -1)
            f_ref[g, PAD - 1:PAD, :] = first * (row(s_ref, g + 1, 0) - row(s_ref, g + 1, -1))
        for i in range(0, span, SUB):
            here = slice(i, i + SUB)
            fluxes = []
            for g in range(G):
                flux = (d_ref[g + 1, at(i + 1), :] + d_ref[g + 1, at(i), :]) * a_ref[g, here, :]
                f_ref[g, at(i), :] = flux
                fluxes.append(flux)
            s, d = s_ref[1, at(i), :], d_ref[1, at(i), :]
            came = (d + d_ref[0, at(i), :]) * (s - s_ref[0, at(i), :])
            for g in range(G):
                s_down, d_down = s_ref[g + 2, at(i), :], d_ref[g + 2, at(i), :]
                goes = (d_down + d) * (s_down - s)
                div = (goes - came) + (fluxes[g] - f_ref[g, at(i - 1), :])
                h = jnp.maximum((h_ref[g, here, :] + m_ref[g, here, :]) + div, 0.0)
                h_ref[g, here, :] = h
                put(s_new, g, i, b_ref[g, here, :] + h)
                came, s, d = goes, s_down, d_down
        for g in range(G):
            wrap(s_new, g)

    def pair(t, carry):
        with jax.named_scope("pair"):
            step(s0_ref, s1_ref)
            step(s1_ref, s0_ref)
        return carry
    lax.fori_loop(0, STEPS // 2, pair, 0)

    with jax.named_scope("back"):
        for g in range(G):
            block = (h_ref[g] * (1.0 / unit)).T
            for j in range(tiles):
                fin[j, pl.ds(g, SUB, stride=G), :] = block[j * SUB:(j + 1) * SUB]
        for j in range(tiles):
            final_ref[:, j * LANES:(j + 1) * LANES] = fin[j, rows:2 * rows, :]
    gives[1].start()
    gives[0].wait()
    gives[1].wait()


def per_device(n, mode_fields, coeff, eigen, map_friction, bed, smb, thickness):
    rows, cols = map_friction.shape
    mode_dev = mode_fields.shape[0]
    B = n // 4
    H = 2 if n <= 16 else 1
    Q = B * H
    modes = coeff.shape[0]
    anywhere = pl.BlockSpec(memory_space=pl.ANY)
    vmem = pl.BlockSpec(memory_space=pltpu.VMEM)
    strip = (rows, cols)
    part = (rows, cols // H)
    tiles = cols // LANES
    G = 3 * rows // SUB
    ext = (tiles, 3 * rows, LANES)
    planes = (G, LANES, LANES)
    padded = (G + 2, LANES + 2 * PAD, LANES)
    assert tiles * SUB == LANES and G * SUB == 3 * rows and STEPS % 2 == 0
    bf = jnp.bfloat16
    dma = pltpu.SemaphoreType.DMA
    outs = pl.pallas_call(
        functools.partial(gather_kernel, n, H),
        out_shape=(pltpu.VMEM(strip, F32),) + (pltpu.VMEM(planes, F32),) * 4,
        in_specs=[pl.BlockSpec(memory_space=pl.ANY)] * 7,
        out_specs=(vmem,) * 5,
        scratch_shapes=[
            pltpu.VMEM((1, modes), F32),
            pltpu.VMEM((1, modes), F32),
        ] + [pltpu.VMEM(strip, F32)] * 4 + [
            dma((6,)),
            pltpu.VMEM((n * H, mode_dev) + part, bf),
            pltpu.VMEM((2 * Q,) + part, F32),
            pltpu.VMEM((2 * Q,) + part, F32),
            pltpu.VMEM((2 * Q,) + part, F32),
            pltpu.VMEM((Q,) + part, WIRE),
            pltpu.VMEM((Q,) + part, WIRE),
            pltpu.VMEM((Q,) + part, WIRE),
            pltpu.VMEM((Q,) + part, WIRE),
            pltpu.VMEM((3,) + strip, bf),
            pltpu.VMEM((2, 3) + strip, bf),
            pltpu.VMEM((3,) + strip, bf),
            pltpu.VMEM((H,) + part, bf),
            pltpu.VMEM((2, H) + part, bf),
        ] + [pltpu.VMEM(ext, F32)] * 4 + [
            dma((n * H,)), dma((2 * Q,)), dma((2 * Q,)), dma((Q,)), dma((Q,)), dma((Q,)), dma((Q,)), dma((2 + 2 * H,)), dma((2 + 2 * H,)), dma((1,)), dma((1,)),
        ],
        compiler_params=pltpu.CompilerParams(collective_id=0, has_side_effects=True, vmem_limit_bytes=58 * 2**20),
        name="posterior_gather",
    )(coeff.reshape(1, modes), eigen.reshape(1, modes), map_friction, bed, smb, thickness, mode_fields)
    return pl.pallas_call(
        step_kernel,
        out_shape=(jax.ShapeDtypeStruct(strip, F32),) * 2,
        in_specs=[vmem] * 5,
        out_specs=(anywhere, anywhere),
        scratch_shapes=[pltpu.VMEM(strip, F32), dma((2,))] + [pltpu.VMEM(planes, F32)] * 2 + [pltpu.VMEM((G, LANES + 2 * PAD, LANES), F32)]
        + [pltpu.VMEM(padded, F32)] * 3 + [pltpu.VMEM(ext, F32)],
        compiler_params=pltpu.CompilerParams(vmem_limit_bytes=16 * 2**20),
        name="ice_steps",
    )(*outs)


def solution(mesh):
    n = mesh.shape["modes"]
    return jax.shard_map(
        functools.partial(per_device, n),
        mesh=mesh,
        in_specs=(
            P(("groups", "modes"), None, None),
            P("groups"),
            P("groups"),
            P(("groups", "modes"), None),
            P(("groups", "modes"), None),
            P(("groups", "modes"), None),
            P(("groups", "modes"), None),
        ),
        out_specs=(P(("groups", "modes"), None), P(("groups", "modes"), None)),
        check_vma=False,
    )
```

time: 31.5 us -> 26.9 us (0.85)
  Pallas kernels: 30.7 us -> 26.1 us
    pallas_call x1, Pallas kernels: 9.07 us -> 4.71 us  [per_device(): pl.pallas_call(step_kernel, out_shape=(jax.ShapeDtypeStruct(strip, F32),)...]
where the time goes in v3:
time: 26.9 us; the launch traced here: 26.8 us
  Pallas kernels  26.1 us (97%)
  between operations  0.64 us (2%)
    pallas_call x1, Pallas kernels, per_device(): pl.pallas_call(functools.partial(gather_kernel, n, H), out_shape=(pltpu.V...  21.4 us
    pallas_call x1, Pallas kernels, per_device(): pl.pallas_call(step_kernel, out_shape=(jax.ShapeDtypeStruct(strip, F32),)...  4.71 us

profile of v3, /device:TPU:1, one launch (start us, length us, event | category | flops | bytes accessed | tf_op | source)
XLA Modules:
  0.0 26.8 jit_solution(2199934817964447115)
XLA Ops:
  0.6 21.4 %posterior_gather.1 = (f32[16,2048]{1,0:T(8,128)S(1)}, f32[6,128,128]{2,1,0:T(8,128)S(1)}, f32[6,128,128]{2,1,0:T(8,128)S(1)}, f32[6,128,128]{2,1,0:T(8,128)S(1)}, f32[6,128,128]{2,1,0:T(8,128)S(1)}) custom-call(f32[1,128]{1,0:T(1,128)} %bitcast.2, f32[1,128]{1,0:T(1,128)} %bitcast.3, f32[16,2048]{1,0:T(8,128)} %map_hbm.1, f32[16,2048]{1,0:T(8,128)} %bed_hbm.1, ...), custom_call_target="tpu_custom_call" | custom-call | tf_op jit(solution)/shard_map/posterior_gather/pallas_call | solution.py:484
  22.0 4.7 %ice_steps.1 = (f32[16,2048]{1,0:T(8,128)}, f32[16,2048]{1,0:T(8,128)}) custom-call(f32[16,2048]{1,0:T(8,128)S(1)} %get-tuple-element.7.logf_ref, f32[6,128,128]{2,1,0:T(8,128)S(1)} %get-tuple-element.8.b_ref, f32[6,128,128]{2,1,0:T(8,128)S(1)} %get-tuple-element.9.e_ref, f32[6,128,128]{2,1,0:T(8,128)S(1)} %get-tuple-element.10.m_ref, ...), custom_call_target="tpu_custom_call" | custom-call | tf_op jit(solution)/shard_map/ice_steps/pallas_call | solution.py:513
